TPU v7x, 32 devices: a whole 2x2x4 slice. The times are simulated.
32 devices in a mesh: groups: 2 (over y), tok: 16 (over z, x, core).
Axes of the slice: x: 2, y: 2, z: 4, core: 2. Of those that a mesh axis runs over, the one named last changes fastest.
Arguments:
- queries: bfloat16 [2048, 2048], P(('groups', 'tok')), parts along dimension 0, may hold values from -256 to 256, as said below
- fresh_keys: bfloat16 [2048, 2048], P(('groups', 'tok')), parts along dimension 0, may hold values from -6 to 6, as said below
- fresh_values: bfloat16 [2048, 2048], P(('groups', 'tok')), parts along dimension 0, may hold values from -6 to 6
- stale_keys: bfloat16 [2048, 2048], P(('groups', 'tok')), parts along dimension 0, may hold values from -6 to 6
- stale_values: bfloat16 [2048, 2048], P(('groups', 'tok')), parts along dimension 0, may hold values from -6 to 6
- patch_starts: int32 [32], P('groups'), parts along dimension 0, may hold values from 0 to 1023, as said below
- order_starts: int32 [32], P('groups'), parts along dimension 0, may hold values from 0 to 1023, as said below
Outputs:
- attended: bfloat16 [2048, 2048], P(('groups', 'tok')), parts along dimension 0
There are 2 independent parts, one for each index of `groups`. A program takes and returns all parts, laid end to end along the dimension named above; each array names one. Nothing has to cross between parts.
Inputs may be any that keep to these rules, and one draw needn't show every extreme that they name: `patch_starts`: strictly increasing; the first entry is 0. `order_starts`: the entries of patch_starts, each once, in processing order. `queries`: entries are finite. `fresh_keys`: entries are finite.
All inputs are finite; a program needn't handle non-finite values.
Results may differ from a plain program's by a relative error of at most 0.0049.
Values may be sent and summed in bfloat16 or wider, within the bound.
A program may use at most 128 MiB of HBM per device.

v0:
```python
import math
import jax
import jax.numpy as jnp
from jax import lax
from jax.sharding import PartitionSpec as P

HEADS = 16
HEAD_DIM = 128


def token_ranks(positions, patch_starts, order_starts):
    patch_count = patch_starts.shape[0]
    slot_ids = jnp.arange(patch_count, dtype=jnp.int32)
    patch_of = jnp.sum((patch_starts[None, :] <= positions[:, None]).astype(jnp.int32), axis=1) - 1
    matches = (order_starts[:, None] == patch_starts[None, :]).astype(jnp.int32)
    rank_of = jnp.sum(matches * slot_ids[:, None], axis=0)
    one_hot = (patch_of[:, None] == slot_ids[None, :]).astype(jnp.int32)
    return jnp.sum(one_hot * rank_of[None, :], axis=1)


def masked_scores(query_block, query_rank, key_stack, key_rank):
    dims = (((1,), (1,)), ((), ()))
    score_scale = 1.0 / math.sqrt(query_block.shape[-1])
    fresh_scores = (
        lax.dot_general(query_block, key_stack[0], dims, preferred_element_type=jnp.float32)
        * score_scale
    )
    stale_scores = (
        lax.dot_general(query_block, key_stack[2], dims, preferred_element_type=jnp.float32)
        * score_scale
    )
    fresh_ok = key_rank[None, :] <= query_rank[:, None]
    fresh_scores = jnp.where(fresh_ok, fresh_scores, -jnp.inf)
    stale_scores = jnp.where(fresh_ok, -jnp.inf, stale_scores)
    return (fresh_scores, stale_scores)


def attend_block(query_block, query_rank, key_stack, key_rank):
    fresh_scores, stale_scores = masked_scores(query_block, query_rank, key_stack, key_rank)
    row_max = jnp.maximum(jnp.max(fresh_scores, axis=1), jnp.max(stale_scores, axis=1))[:, None]
    fresh_exp = jnp.exp(fresh_scores - row_max)
    stale_exp = jnp.exp(stale_scores - row_max)
    row_total = jnp.sum(fresh_exp, axis=1, keepdims=True) + jnp.sum(
        stale_exp, axis=1, keepdims=True
    )
    fresh_probs = (fresh_exp / row_total).astype(jnp.bfloat16)
    stale_probs = (stale_exp / row_total).astype(jnp.bfloat16)
    mixed = jnp.dot(fresh_probs, key_stack[1], preferred_element_type=jnp.float32)
    mixed = mixed + jnp.dot(stale_probs, key_stack[3], preferred_element_type=jnp.float32)
    return mixed.astype(jnp.bfloat16)


def attend_rows(query_rows, query_rank, key_stack, key_rank):
    row_count = query_rows.shape[0]
    block_rows = 512
    blocks = row_count // block_rows

    def one_block(inputs):
        return attend_block(inputs[0], inputs[1], key_stack, key_rank)

    result = lax.map(
        one_block,
        (
            query_rows.reshape(blocks, block_rows, query_rows.shape[1]),
            query_rank.reshape(blocks, block_rows),
        ),
    )
    return result.reshape(row_count, query_rows.shape[1])


def shards(queries, fresh_keys, fresh_values, stale_keys, stale_values, patch_starts, order_starts):
    devices = lax.axis_size("tok")
    tok_dev, row_width = queries.shape
    group_size = devices // HEADS
    slab_rows = tok_dev // group_size
    my_index = lax.axis_index("tok")
    member = my_index % group_size
    query_slabs = (
        queries.reshape(group_size, slab_rows, HEADS, HEAD_DIM)
        .transpose(2, 0, 1, 3)
        .reshape(devices, slab_rows, HEAD_DIM)
    )
    query_rows = lax.all_to_all(query_slabs, "tok", split_axis=0, concat_axis=0, tiled=True)
    stacked = jnp.stack([fresh_keys, fresh_values, stale_keys, stale_values]).reshape(
        4, tok_dev, HEADS, HEAD_DIM
    )
    sender_base = jnp.arange(devices, dtype=jnp.int32)[:, None] * tok_dev
    slab_offsets = jnp.arange(slab_rows, dtype=jnp.int32)[None, :]
    query_pos = (sender_base + member * slab_rows + slab_offsets).reshape(-1)
    by_head = stacked.transpose(0, 2, 1, 3)[:, :, None]
    spread = jnp.broadcast_to(by_head, (4, HEADS, group_size, tok_dev, HEAD_DIM)).reshape(
        4, devices, tok_dev, HEAD_DIM
    )
    arrived = lax.all_to_all(spread, "tok", split_axis=1, concat_axis=1, tiled=True)
    key_stack = arrived.reshape(4, devices * tok_dev, HEAD_DIM)
    key_rank = token_ranks(
        jnp.arange(devices * tok_dev, dtype=jnp.int32), patch_starts, order_starts
    )
    query_rank = token_ranks(query_pos, patch_starts, order_starts)
    attended = attend_rows(
        query_rows.reshape(devices * slab_rows, HEAD_DIM), query_rank, key_stack, key_rank
    )
    returned = lax.all_to_all(
        attended.reshape(devices, slab_rows, HEAD_DIM),
        "tok",
        split_axis=0,
        concat_axis=0,
        tiled=True,
    )
    return (
        returned.reshape(HEADS, group_size, slab_rows, HEAD_DIM)
        .transpose(1, 2, 0, 3)
        .reshape(tok_dev, row_width)
    )


def solution(mesh):
    placed = (
        P(("groups", "tok"), None),
        P(("groups", "tok"), None),
        P(("groups", "tok"), None),
        P(("groups", "tok"), None),
        P(("groups", "tok"), None),
        P("groups"),
        P("groups"),
    )
    return jax.shard_map(
        shards, mesh=mesh, in_specs=placed, out_specs=P(("groups", "tok"), None), check_vma=False
    )
```

profile of v0, /device:TPU:0, one launch (start us, length us, event | category | flops | bytes accessed | tf_op | source)
XLA Modules:
  0.0 72.3 jit_solution(15579702160136215881)
XLA Ops:
  0.0 1.0 %copy.24 = bf16[8,8,16,128]{3,2,1,0:T(8,128)(2,1)S(1)} copy(bf16[8,8,16,128]{3,1,2,0:T(8,128)(2,1)} %bitcast.87) | data formatting | bytes 524288
  1.0 1.0 %copy.25 = bf16[8,8,16,128]{3,2,1,0:T(8,128)(2,1)S(1)} copy(bf16[8,8,16,128]{3,1,2,0:T(8,128)(2,1)} %bitcast.88) | data formatting | bytes 524288
  2.0 1.0 %copy.26 = bf16[8,8,16,128]{3,2,1,0:T(8,128)(2,1)S(1)} copy(bf16[8,8,16,128]{3,1,2,0:T(8,128)(2,1)} %bitcast.89) | data formatting | bytes 524288
  3.0 1.0 %copy.27 = bf16[8,8,16,128]{3,2,1,0:T(8,128)(2,1)S(1)} copy(bf16[8,8,16,128]{3,1,2,0:T(8,128)(2,1)} %bitcast.90) | data formatting | bytes 524288
  4.1 1.3 %copy.20 = bf16[4,16,64,128]{3,2,0,1:T(8,128)(2,1)} copy(bf16[4,16,64,128]{3,1,2,0:T(8,128)(2,1)S(1)} %maximum_bitcast_fusion) | data formatting | bytes 2097152 | tf_op jit(solution)/shard_map/transpose | solution.py:90
  5.4 7.5 %all-to-all-start.1 = ((bf16[4,16,64,128]{3,2,0,1:T(8,128)(2,1)}), bf16[4,16,64,128]{3,2,0,1:T(8,128)(2,1)S(1)}, u32[]{:S(2)}, u32[]{:S(2)}) async-start(bf16[4,16,64,128]{3,2,0,1:T(8,128)(2,1)} %copy.20), calls=%async_computation.1 | async-start | bytes 2097152 | tf_op jit(solution)/shard_map/all_to_all | solution.py:94
  13.0 0.8 %copy.32 = bf16[1,64,16,128]{3,1,2,0:T(8,128)(2,1)} copy(bf16[1,64,16,128]{3,2,1,0:T(8,128)(2,1)S(1)} %bitcast.82) | data formatting | bytes 524288 | tf_op jit(solution)/shard_map/reshape | solution.py:79
  13.8 22.0 %all-to-all-done.1 = bf16[4,16,64,128]{3,2,0,1:T(8,128)(2,1)S(1)} async-done(((bf16[4,16,64,128]{3,2,0,1:T(8,128)(2,1)}), bf16[4,16,64,128]{3,2,0,1:T(8,128)(2,1)S(1)}, u32[]{:S(2)}, u32[]{:S(2)}) %all-to-all-start.1) | async-done | bytes 1048608 | tf_op jit(solution)/shard_map/all_to_all | solution.py:94
  35.8 6.8 %all-to-all-start = ((bf16[16,64,128]{2,1,0:T(8,128)(2,1)}), bf16[16,64,128]{2,1,0:T(8,128)(2,1)S(1)}, u32[]{:S(2)}, u32[]{:S(2)}) async-start(bf16[16,64,128]{2,1,0:T(8,128)(2,1)} %bitcast.62), calls=%async_computation | async-start | bytes 524288 | tf_op jit(solution)/shard_map/all_to_all | solution.py:83
  43.1 9.5 %all-to-all-done = bf16[16,64,128]{2,1,0:T(8,128)(2,1)S(1)} async-done(((bf16[16,64,128]{2,1,0:T(8,128)(2,1)}), bf16[16,64,128]{2,1,0:T(8,128)(2,1)S(1)}, u32[]{:S(2)}, u32[]{:S(2)}) %all-to-all-start) | async-done | bytes 262176 | tf_op jit(solution)/shard_map/all_to_all | solution.py:83
  52.6 6.0 %while.10 = (s32[]{:T(128)}, bf16[2,512,128]{2,1,0:T(8,128)(2,1)S(1)}, s32[1024]{0:T(1024)S(1)}, s32[2,512]{1,0:T(2,128)S(1)}, bf16[2,512,128]{2,1,0:T(8,128)(2,...) while((s32[]{:T(128)}, bf16[2,512,128]{2,1,0:T(8,128)(2,1)S(1)}, s32[1024]{0:T(1024)S(1)}, ...), condition=%wide.region_10.11_spmd, body=%wide.region_5.10_spmd.sunk | while | flops 546438144 | bytes 14596189 | solution.py:61
  52.6 0.5 fusion.31
  53.2 0.5 fusion.32
  53.7 0.7 fusion.33
  54.4 0.6 fusion.34
  55.0 0.6 fusion.35
  55.7 0.5 fusion.31
  56.2 0.5 fusion.32
  56.7 0.7 fusion.33
  57.5 0.6 fusion.34
  58.0 0.6 fusion.35
  58.7 12.7 %all_to_all.15 = bf16[16,64,128]{2,1,0:T(8,128)(2,1)S(1)} all-to-all(bf16[16,64,128]{2,1,0:T(8,128)(2,1)S(1)} %bitcast.93), channel_id=1, replica_groups=mesh['groups'=2,'tok'=16] {'tok'}, dimensions={0} | all-to-all | bytes 524288 | tf_op jit(solution)/shard_map/all_to_all | solution.py:103
  71.3 0.2 copy.22
  71.5 0.8 %copy.31 = bf16[8,8,16,128]{3,1,2,0:T(8,128)(2,1)} copy(bf16[8,8,16,128]{3,2,1,0:T(8,128)(2,1)S(1)} %bitcast.81) | data formatting | bytes 524288
  (24 shorter events, 0.8 us)
Async XLA Ops:
  4.1 8.8 %copy-start = (bf16[64,2048]{1,0:T(8,128)(2,1)S(1)}, bf16[64,2048]{1,0:T(8,128)(2,1)}, u32[]{:S(2)}) copy-start(bf16[64,2048]{1,0:T(8,128)(2,1)} %param.9) | copy-start | bytes 786436
  5.4 37.2 %copy-start.1 = (s32[16]{0:T(128)S(1)}, s32[16]{0:T(128)}, u32[]{:S(2)}) copy-start(s32[16]{0:T(128)} %param.14) | copy-start | bytes 196
  5.4 37.2 %copy-start.2 = (s32[16]{0:T(128)S(1)}, s32[16]{0:T(128)}, u32[]{:S(2)}) copy-start(s32[16]{0:T(128)} %param.15) | copy-start | bytes 196
  5.4 30.4 %all-to-all-start.1 = ((bf16[4,16,64,128]{3,2,0,1:T(8,128)(2,1)}), bf16[4,16,64,128]{3,2,0,1:T(8,128)(2,1)S(1)}, u32[]{:S(2)}, u32[]{:S(2)}) async-start(bf16[4,16,64,128]{3,2,0,1:T(8,128)(2,1)} %copy.20), calls=%async_computation.1 | async-start | bytes 2097152 | tf_op jit(solution)/shard_map/all_to_all | solution.py:94
  35.8 16.8 %all-to-all-start = ((bf16[16,64,128]{2,1,0:T(8,128)(2,1)}), bf16[16,64,128]{2,1,0:T(8,128)(2,1)S(1)}, u32[]{:S(2)}, u32[]{:S(2)}) async-start(bf16[16,64,128]{2,1,0:T(8,128)(2,1)} %bitcast.62), calls=%async_computation | async-start | bytes 524288 | tf_op jit(solution)/shard_map/all_to_all | solution.py:83
where the time goes:
time: 72.7 us; the launch traced here: 72.3 us
  waiting for transfers between devices  31.5 us (43%)
  starting transfers between devices  14.3 us (20%)
  blocking collectives  12.7 us (17%)
  local copies, waits for them, and re-layouts  7.16 us (10%)
  matrix products  4.5 us (6%)
  other arithmetic  1.96 us (3%)
    all_to_all x1, waiting for transfers between devices, shards(): lax.all_to_all(spread, 'tok', split_axis=1, concat_axis=1, tiled=True)  22 us
    all_to_all x1, blocking collectives, shards(): lax.all_to_all(attended.reshape(devices, slab_rows, HEAD_DIM), 'tok', spl...  12.7 us
    all_to_all x1, waiting for transfers between devices, shards(): lax.all_to_all(query_slabs, 'tok', split_axis=0, concat_axis=0, tiled=True)  9.51 us
    all_to_all x1, starting transfers between devices, shards(): lax.all_to_all(spread, 'tok', split_axis=1, concat_axis=1, tiled=True)  7.52 us
    all_to_all x1, starting transfers between devices, shards(): lax.all_to_all(query_slabs, 'tok', split_axis=0, concat_axis=0, tiled=True)  6.79 us
    unnamed x12, local copies, waits for them, and re-layouts  4.77 us
  transfers between devices with their start and end apart: 2, of which 2 were waited for; matrix products, arithmetic and copies ran while one was open for 2% of the time, Pallas kernels for 0%

commit v1 on v0

--- a/solution.py
+++ b/solution.py
@@ -91,7 +91,10 @@
     spread = jnp.broadcast_to(by_head, (4, HEADS, group_size, tok_dev, HEAD_DIM)).reshape(
         4, devices, tok_dev, HEAD_DIM
     )
-    arrived = lax.all_to_all(spread, "tok", split_axis=1, concat_axis=1, tiled=True)
+    arrived = jnp.concatenate(
+        lax.all_to_all(jnp.stack(jnp.split(spread, lax.axis_size("tok"), axis=1)), "tok", 0, 0),
+        axis=1,
+    )
     key_stack = arrived.reshape(4, devices * tok_dev, HEAD_DIM)
     key_rank = token_ranks(
         jnp.arange(devices * tok_dev, dtype=jnp.int32), patch_starts, order_starts

time: 72.7 us -> 83.8 us (1.15)
  local copies, waits for them, and re-layouts: 7.16 us -> 18.4 us
    unnamed x12 -> x27, local copies, waits for them, and re-layouts: 4.77 us -> 14.2 us
    split x0 -> x1, local copies, waits for them, and re-layouts: none -> 2.41 us  [shards(): jnp.split(spread, lax.axis_size('tok'), axis=1)]
    transpose x1 -> x0, local copies, waits for them, and re-layouts: 1.26 us -> none  [shards(): by_head = stacked.transpose(0, 2, 1, 3)[:, :, None]]
where the time goes in v1:
time: 83.8 us; the launch traced here: 83.4 us
  waiting for transfers between devices  31.5 us (38%)
  local copies, waits for them, and re-layouts  18.4 us (22%)
  starting transfers between devices  14.2 us (17%)
  blocking collectives  12.7 us (15%)
  matrix products  4.5 us (5%)
  other arithmetic  1.96 us (2%)
    all_to_all x1, waiting for transfers between devices, shards(): lax.all_to_all(jnp.stack(jnp.split(spread, lax.axis_size('tok'), axis=1))...  22 us
    unnamed x27, local copies, waits for them, and re-layouts  14.2 us
    all_to_all x1, blocking collectives, shards(): lax.all_to_all(attended.reshape(devices, slab_rows, HEAD_DIM), 'tok', spl...  12.7 us
    all_to_all x1, waiting for transfers between devices, shards(): lax.all_to_all(query_slabs, 'tok', split_axis=0, concat_axis=0, tiled=True)  9.51 us
    all_to_all x1, starting transfers between devices, shards(): lax.all_to_all(jnp.stack(jnp.split(spread, lax.axis_size('tok'), axis=1))...  7.39 us
    all_to_all x1, starting transfers between devices, shards(): lax.all_to_all(query_slabs, 'tok', split_axis=0, concat_axis=0, tiled=True)  6.79 us
    split x1, local copies, waits for them, and re-layouts, shards(): jnp.split(spread, lax.axis_size('tok'), axis=1)  2.41 us
  transfers between devices with their start and end apart: 2, of which 2 were waited for; matrix products, arithmetic and copies ran while one was open for 2% of the time, Pallas kernels for 0%

profile of v1, /device:TPU:0, one launch (start us, length us, event | category | flops | bytes accessed | tf_op | source)
XLA Modules:
  0.0 83.4 jit_solution(10716623988944800960)
XLA Ops:
  0.0 1.0 %copy.221 = bf16[8,8,16,128]{3,2,1,0:T(8,128)(2,1)S(1)} copy(bf16[8,8,16,128]{3,1,2,0:T(8,128)(2,1)} %bitcast.121) | data formatting | bytes 524288
  1.0 1.0 %copy.222 = bf16[8,8,16,128]{3,2,1,0:T(8,128)(2,1)S(1)} copy(bf16[8,8,16,128]{3,1,2,0:T(8,128)(2,1)} %bitcast.122) | data formatting | bytes 524288
  2.0 1.0 %copy.223 = bf16[8,8,16,128]{3,2,1,0:T(8,128)(2,1)S(1)} copy(bf16[8,8,16,128]{3,1,2,0:T(8,128)(2,1)} %bitcast.123) | data formatting | bytes 524288
  3.0 1.0 %copy.224 = bf16[8,8,16,128]{3,2,1,0:T(8,128)(2,1)S(1)} copy(bf16[8,8,16,128]{3,1,2,0:T(8,128)(2,1)} %bitcast.124) | data formatting | bytes 524288
  4.1 2.4 %fusion.22 = (bf16[4,1,64,128]{3,1,2,0:T(2,128)(2,1)S(1)}, bf16[4,1,64,128]{3,1,2,0:T(2,128)(2,1)S(1)}, bf16[4,1,64,128]{3,1,2,0:T(2,128)(2,1)S(1)}, bf16[4,1,64...) fusion(bf16[4,16,64,128]{3,1,2,0:T(8,128)(2,1)S(1)} %maximum_bi, ...), kind=kLoop, calls=%fused_computation.61 | loop fusion | bytes 2097152 | tf_op jit(solution)/shard_map/split | solution.py:95
  6.5 0.6 bitcast_dynamic-update-slice_fusion.15
  7.8 0.6 bitcast_dynamic-update-slice_fusion.13
  9.7 0.6 bitcast_dynamic-update-slice_fusion.10
  10.3 0.6 bitcast_dynamic-update-slice_fusion.9
  11.6 0.6 bitcast_dynamic-update-slice_fusion.7
  12.2 0.6 bitcast_dynamic-update-slice_fusion.6
  12.8 0.6 bitcast_dynamic-update-slice_fusion.5
  15.3 0.6 bitcast_dynamic-update-slice_fusion.1
  16.0 0.6 bitcast_dynamic-update-slice_fusion
  16.6 7.4 %all-to-all-start.1 = ((bf16[16,4,1,64,128]{4,3,1,2,0:T(8,128)(2,1)}), bf16[16,4,1,64,128]{4,3,1,2,0:T(8,128)(2,1)S(1)}, u32[]{:S(2)}, u32[]{:S(2)}) async-start(bf16[16,4,1,64,128]{4,3,1,2,0:T(8,128)(2,1)} %bitcast_dynamic-update-slice_fusion), calls=%async_computation.1 | async-start | bytes 2097152 | tf_op jit(solution)/shard_map/all_to_all | solution.py:95
  24.1 0.8 copy.245
  24.9 22.0 %all-to-all-done.1 = bf16[16,4,1,64,128]{4,3,1,2,0:T(8,128)(2,1)S(1)} async-done(((bf16[16,4,1,64,128]{4,3,1,2,0:T(8,128)(2,1)}), bf16[16,4,1,64,128]{4,3,1,2,0:T(8,128)(2,1)S(1)}, u32[]{:S(2)}, u32[]{:S(2)}) %all-to-all-start.1) | async-done | bytes 1048608 | tf_op jit(solution)/shard_map/all_to_all | solution.py:95
  46.9 6.8 %all-to-all-start = ((bf16[16,64,128]{2,1,0:T(8,128)(2,1)}), bf16[16,64,128]{2,1,0:T(8,128)(2,1)S(1)}, u32[]{:S(2)}, u32[]{:S(2)}) async-start(bf16[16,64,128]{2,1,0:T(8,128)(2,1)} %bitcast.96), calls=%async_computation | async-start | bytes 524288 | tf_op jit(solution)/shard_map/all_to_all | solution.py:83
  54.2 9.5 %all-to-all-done = bf16[16,64,128]{2,1,0:T(8,128)(2,1)S(1)} async-done(((bf16[16,64,128]{2,1,0:T(8,128)(2,1)}), bf16[16,64,128]{2,1,0:T(8,128)(2,1)S(1)}, u32[]{:S(2)}, u32[]{:S(2)}) %all-to-all-start) | async-done | bytes 262176 | tf_op jit(solution)/shard_map/all_to_all | solution.py:83
  63.7 6.0 %while.10 = (s32[]{:T(128)}, bf16[2,512,128]{2,1,0:T(8,128)(2,1)S(1)}, s32[1024]{0:T(1024)S(1)}, s32[2,512]{1,0:T(2,128)S(1)}, bf16[2,512,128]{2,1,0:T(8,128)(2,...) while((s32[]{:T(128)}, bf16[2,512,128]{2,1,0:T(8,128)(2,1)S(1)}, s32[1024]{0:T(1024)S(1)}, ...), condition=%wide.region_10.11_spmd, body=%wide.region_5.10_spmd.sunk | while | flops 546438144 | bytes 14596189 | solution.py:61
  64.8 0.7 fusion.34
  67.8 0.7 fusion.34
  69.7 12.7 %all_to_all.15 = bf16[16,64,128]{2,1,0:T(8,128)(2,1)S(1)} all-to-all(bf16[16,64,128]{2,1,0:T(8,128)(2,1)S(1)} %bitcast.127), channel_id=1, replica_groups=mesh['groups'=2,'tok'=16] {'tok'}, dimensions={0} | all-to-all | bytes 524288 | tf_op jit(solution)/shard_map/all_to_all | solution.py:106
  82.6 0.8 copy.244
  (40 shorter events, 9.8 us)
Async XLA Ops:
  9.7 14.3 %copy-start = (bf16[64,2048]{1,0:T(8,128)(2,1)S(1)}, bf16[64,2048]{1,0:T(8,128)(2,1)}, u32[]{:S(2)}) copy-start(bf16[64,2048]{1,0:T(8,128)(2,1)} %param.9) | copy-start | bytes 786436
  14.7 39.0 %copy-start.1 = (s32[16]{0:T(128)S(1)}, s32[16]{0:T(128)}, u32[]{:S(2)}) copy-start(s32[16]{0:T(128)} %param.14) | copy-start | bytes 196
  14.7 39.0 %copy-start.2 = (s32[16]{0:T(128)S(1)}, s32[16]{0:T(128)}, u32[]{:S(2)}) copy-start(s32[16]{0:T(128)} %param.15) | copy-start | bytes 196
  16.6 30.3 %all-to-all-start.1 = ((bf16[16,4,1,64,128]{4,3,1,2,0:T(8,128)(2,1)}), bf16[16,4,1,64,128]{4,3,1,2,0:T(8,128)(2,1)S(1)}, u32[]{:S(2)}, u32[]{:S(2)}) async-start(bf16[16,4,1,64,128]{4,3,1,2,0:T(8,128)(2,1)} %bitcast_dynamic-update-slice_fusion), calls=%async_computation.1 | async-start | bytes 2097152 | tf_op jit(solution)/shard_map/all_to_all | solution.py:95
  46.9 16.8 %all-to-all-start = ((bf16[16,64,128]{2,1,0:T(8,128)(2,1)}), bf16[16,64,128]{2,1,0:T(8,128)(2,1)S(1)}, u32[]{:S(2)}, u32[]{:S(2)}) async-start(bf16[16,64,128]{2,1,0:T(8,128)(2,1)} %bitcast.96), calls=%async_computation | async-start | bytes 524288 | tf_op jit(solution)/shard_map/all_to_all | solution.py:83
